TPU v7x, 32 devices: a whole 2x2x4 slice. The times are simulated.
32 devices in a mesh: dp: 4 (over z), mp: 8 (over y, x, core).
Axes of the slice: x: 2, y: 2, z: 4, core: 2. Of those that a mesh axis runs over, the one named last changes fastest.
Arguments:
- tokens: bfloat16 [8192, 2048], P(('dp', 'mp')), may hold values from -6 to 6
- segment: int32 [8192], P('dp'), may hold values from 0 to 2, as said below
- valid: int32 [8192], replicated, may hold values from 0 to 1
- gain_attn: float32 [2048], replicated, may hold values from 0.5 to 1.5
- w_query: bfloat16 [2048, 2048], P(None, 'mp'), may hold values from -0.125 to 0.125
- w_key: bfloat16 [2048, 2048], P(None, 'mp'), may hold values from -0.125 to 0.125
- w_value: bfloat16 [2048, 2048], P(None, 'mp'), may hold values from -0.125 to 0.125
- w_out: bfloat16 [2048, 2048], P('mp'), may hold values from -3 to 3
- gain_mlp: float32 [2048], replicated, may hold values from 0.5 to 1.5
- w_up: bfloat16 [2048, 8192], P(None, 'mp'), may hold values from -0.125 to 0.125
- w_down: bfloat16 [8192, 2048], P('mp'), may hold values from -0.0625 to 0.0625
- grad_out: bfloat16 [8192, 2048], P(('dp', 'mp')), may hold values from -6 to 6
Outputs:
- out_tokens: bfloat16 [8192, 2048], P(('dp', 'mp'))
- grad_tokens: bfloat16 [8192, 2048], P(('dp', 'mp'))
- grad_gain_attn: float32 [2048], P(('dp', 'mp'))
- grad_query: float32 [2048, 2048], P('dp', 'mp')
- grad_key: float32 [2048, 2048], P('dp', 'mp')
- grad_value: float32 [2048, 2048], P('dp', 'mp')
- grad_out_proj: float32 [2048, 2048], P('mp', 'dp')
- grad_gain_mlp: float32 [2048], P(('dp', 'mp'))
- grad_up: float32 [2048, 8192], P('dp', 'mp')
- grad_down: float32 [8192, 2048], P('mp', 'dp')
- rms_stream: float32 [], replicated
- rms_attn: float32 [], replicated
- rms_mlp: float32 [], replicated
Inputs may be any that keep to these rules, and one draw needn't show every extreme that they name: `segment`: within each slot the clip numbers never fall; clip 1 starts before position 128 of the slot and clip 2 starts at or after position 1921.
All inputs are finite; a program needn't handle non-finite values.
Results may differ from a plain program's by a relative error of at most 0.022.
Values may be sent and summed in bfloat16 or wider, within the bound.
A program may use at most 512 MiB of HBM per device.

v0:
```python
import jax
import jax.numpy as jnp
from jax import lax
from jax.sharding import PartitionSpec as P

D = 2048
HD = 128
EPSILON = 1e-05
NEGATIVE = -1e30


def norm_rows(values, norm_gain):
    scale = lax.rsqrt(jnp.mean(values * values, axis=-1, keepdims=True) + EPSILON)
    return values * scale * norm_gain


def norm_back(values, norm_gain, grad_norm):
    scale = lax.rsqrt(jnp.mean(values * values, axis=-1, keepdims=True) + EPSILON)
    normal = values * scale
    grad_hat = grad_norm * norm_gain
    inner = jnp.mean(grad_hat * normal, axis=-1, keepdims=True)
    return (scale * (grad_hat - normal * inner), normal)


def gelu_fn(values):
    return jax.nn.gelu(values, approximate=True)


def contract_rows(left_side, right_side):
    return lax.dot_general(
        left_side, right_side, (((0,), (0,)), ((), ())), preferred_element_type=jnp.float32
    )


def contract_cols(left_side, right_side):
    return lax.dot_general(
        left_side, right_side, (((1,), (1,)), ((), ())), preferred_element_type=jnp.float32
    )


def block_mask(first_row, row_count, segment_rows, valid_rows):
    rows_here = first_row + jnp.arange(row_count, dtype=jnp.int32)
    columns = jnp.arange(segment_rows.shape[0], dtype=jnp.int32)
    segment_here = lax.dynamic_slice_in_dim(segment_rows, first_row, row_count)
    same_clip = segment_here[:, None] == segment_rows[None, :]
    earlier = (columns[None, :] < rows_here[:, None]) & (valid_rows[None, :] > 0)
    itself = columns[None, :] == rows_here[:, None]
    return same_clip & (earlier | itself)


def attend_forward(queries, keys_all, values_all, segment_rows, valid_rows, head_count):
    seq_rows = queries.shape[0]
    block_rows = min(512, seq_rows)
    key_heads = keys_all.reshape(seq_rows, head_count, HD)
    value_heads = values_all.reshape(seq_rows, head_count, HD)

    def one_block(first_row):
        query_block = lax.dynamic_slice_in_dim(queries, first_row, block_rows, 0).reshape(
            block_rows, head_count, HD
        )
        scores = jnp.einsum(
            "qhd,khd->hqk", query_block, key_heads, preferred_element_type=jnp.float32
        ) * HD ** (-0.5)
        allowed = block_mask(first_row, block_rows, segment_rows, valid_rows)
        scores = jnp.where(allowed[None], scores, NEGATIVE)
        largest = jnp.max(scores, axis=-1, keepdims=True)
        powers = jnp.exp(scores - largest)
        row_total = jnp.sum(powers, axis=-1, keepdims=True)
        attention = (powers / row_total).astype(jnp.bfloat16)
        blended = jnp.einsum(
            "hqk,khd->qhd", attention, value_heads, preferred_element_type=jnp.float32
        )
        return (
            blended.astype(jnp.bfloat16).reshape(block_rows, head_count * HD),
            (largest + jnp.log(row_total))[:, :, 0],
        )

    starts = jnp.arange(seq_rows // block_rows, dtype=jnp.int32) * block_rows
    blended, logsum = lax.map(one_block, starts)
    return (blended.reshape(seq_rows, head_count * HD), logsum)


def attend_backward(
    queries, keys_all, values_all, logsum, grad_mixed, segment_rows, valid_rows, head_count
):
    seq_rows = queries.shape[0]
    block_rows = min(512, seq_rows)
    scale = HD ** (-0.5)
    key_heads = keys_all.reshape(seq_rows, head_count, HD)
    value_heads = values_all.reshape(seq_rows, head_count, HD)

    def one_block(running, block_item):
        grad_keys, grad_values = running
        first_row, block_logsum = block_item
        query_block = lax.dynamic_slice_in_dim(queries, first_row, block_rows, 0).reshape(
            block_rows, head_count, HD
        )
        grad_block = lax.dynamic_slice_in_dim(grad_mixed, first_row, block_rows, 0).reshape(
            block_rows, head_count, HD
        )
        scores = (
            jnp.einsum("qhd,khd->hqk", query_block, key_heads, preferred_element_type=jnp.float32)
            * scale
        )
        allowed = block_mask(first_row, block_rows, segment_rows, valid_rows)
        scores = jnp.where(allowed[None], scores, NEGATIVE)
        attention = jnp.exp(scores - block_logsum[:, :, None])
        grad_attention = jnp.einsum(
            "qhd,khd->hqk", grad_block, value_heads, preferred_element_type=jnp.float32
        )
        inner = jnp.sum(grad_attention * attention, axis=-1, keepdims=True)
        grad_scores = (attention * (grad_attention - inner)).astype(jnp.bfloat16)
        grad_query_block = (
            jnp.einsum("hqk,khd->qhd", grad_scores, key_heads, preferred_element_type=jnp.float32)
            * scale
        )
        grad_keys = (
            grad_keys
            + jnp.einsum(
                "hqk,qhd->khd", grad_scores, query_block, preferred_element_type=jnp.float32
            )
            * scale
        )
        grad_values = grad_values + jnp.einsum(
            "hqk,qhd->khd",
            attention.astype(jnp.bfloat16),
            grad_block,
            preferred_element_type=jnp.float32,
        )
        return ((grad_keys, grad_values), grad_query_block.reshape(block_rows, head_count * HD))

    starts = jnp.arange(seq_rows // block_rows, dtype=jnp.int32) * block_rows
    zeros_heads = jnp.zeros((seq_rows, head_count, HD), jnp.float32)
    (grad_keys, grad_values), grad_queries = lax.scan(
        one_block, (zeros_heads, zeros_heads), (starts, logsum)
    )
    width = head_count * HD
    return (
        grad_queries.reshape(seq_rows, width).astype(jnp.bfloat16),
        grad_keys.reshape(seq_rows, width).astype(jnp.bfloat16),
        grad_values.reshape(seq_rows, width).astype(jnp.bfloat16),
    )


def on_device(
    tokens,
    segment,
    valid,
    gain_attn,
    w_query,
    w_key,
    w_value,
    w_out,
    gain_mlp,
    w_up,
    w_down,
    grad_out,
):
    own_rows = tokens.shape[0]
    seq_rows = segment.shape[0]
    head_count = w_query.shape[1] // HD
    dp_index = lax.axis_index("dp")
    mp_index = lax.axis_index("mp")
    own_first = mp_index * own_rows
    valid_group = lax.dynamic_slice_in_dim(valid, dp_index * seq_rows, seq_rows)
    valid_own = lax.dynamic_slice_in_dim(valid_group, own_first, own_rows)
    token_values = tokens.astype(jnp.float32)
    gathered = lax.all_gather(tokens, "mp", axis=0, tiled=True)
    normed_attn = norm_rows(gathered.astype(jnp.float32), gain_attn).astype(jnp.bfloat16)
    queries = jnp.dot(normed_attn, w_query, preferred_element_type=jnp.float32).astype(jnp.bfloat16)
    keys_all = jnp.dot(normed_attn, w_key, preferred_element_type=jnp.float32).astype(jnp.bfloat16)
    values_all = jnp.dot(normed_attn, w_value, preferred_element_type=jnp.float32).astype(
        jnp.bfloat16
    )
    mixed, logsum = attend_forward(queries, keys_all, values_all, segment, valid_group, head_count)
    attn_rows = lax.psum(
        jnp.dot(mixed, w_out, preferred_element_type=jnp.float32).astype(jnp.bfloat16), "mp"
    ).astype(jnp.float32)
    residual_rows = gathered.astype(jnp.float32) + attn_rows
    attn_own = lax.dynamic_slice_in_dim(attn_rows, own_first, own_rows, 0)
    residual_own = lax.dynamic_slice_in_dim(residual_rows, own_first, own_rows, 0)
    normed_mlp = norm_rows(residual_rows, gain_mlp).astype(jnp.bfloat16)
    hidden_pre = jnp.dot(normed_mlp, w_up, preferred_element_type=jnp.float32)
    hidden = gelu_fn(hidden_pre).astype(jnp.bfloat16)
    mlp_own = lax.psum_scatter(
        jnp.dot(hidden, w_down, preferred_element_type=jnp.float32).astype(jnp.bfloat16),
        "mp",
        scatter_dimension=0,
        tiled=True,
    ).astype(jnp.float32)
    stream_own = residual_own + mlp_own
    out_tokens = stream_own.astype(jnp.bfloat16)
    mask_own = valid_own.astype(jnp.float32)[:, None]
    squares = lax.psum(
        (
            jnp.sum(mask_own * stream_own * stream_own),
            jnp.sum(mask_own * attn_own * attn_own),
            jnp.sum(mask_own * mlp_own * mlp_own),
        ),
        ("dp", "mp"),
    )
    counted = jnp.maximum(jnp.sum(valid).astype(jnp.float32) * D, 1.0)
    grad_rows = lax.all_gather(grad_out, "mp", axis=0, tiled=True)
    grad_hidden = contract_cols(grad_rows, w_down)
    grad_down = contract_rows(hidden, grad_rows)
    grad_pre = jax.vjp(gelu_fn, hidden_pre)[1](grad_hidden)[0].astype(jnp.bfloat16)
    grad_up = contract_rows(normed_mlp, grad_pre)
    grad_normed = lax.psum(contract_cols(grad_pre, w_up).astype(jnp.bfloat16), "mp").astype(
        jnp.float32
    )
    grad_input_rows, normal_rows = norm_back(residual_rows, gain_mlp, grad_normed)
    grad_resid_rows = grad_rows.astype(jnp.float32) + grad_input_rows
    grad_resid_own = lax.dynamic_slice_in_dim(grad_resid_rows, own_first, own_rows, 0)
    gain_mlp_part = jnp.sum(
        lax.dynamic_slice_in_dim(grad_normed * normal_rows, own_first, own_rows, 0), axis=0
    )
    grad_branch = grad_resid_rows.astype(jnp.bfloat16)
    grad_out_proj = contract_rows(mixed, grad_branch)
    grad_mixed = contract_cols(grad_branch, w_out).astype(jnp.bfloat16)
    grad_queries, grad_keys, grad_values = attend_backward(
        queries, keys_all, values_all, logsum, grad_mixed, segment, valid_group, head_count
    )
    grad_query = contract_rows(normed_attn, grad_queries)
    grad_key = contract_rows(normed_attn, grad_keys)
    grad_value = contract_rows(normed_attn, grad_values)
    total_term = contract_cols(grad_queries, w_query)
    total_term = total_term + contract_cols(grad_keys, w_key)
    grad_normed_attn = lax.psum_scatter(
        (total_term + contract_cols(grad_values, w_value)).astype(jnp.bfloat16),
        "mp",
        scatter_dimension=0,
        tiled=True,
    ).astype(jnp.float32)
    grad_input_attn, normal_attn = norm_back(token_values, gain_attn, grad_normed_attn)
    grad_tokens = (grad_resid_own + grad_input_attn).astype(jnp.bfloat16)
    gain_attn_part = jnp.sum(grad_normed_attn * normal_attn, axis=0)
    gain_grads = (
        lax.psum_scatter(gain_attn_part, ("dp", "mp"), scatter_dimension=0, tiled=True),
        lax.psum_scatter(gain_mlp_part, ("dp", "mp"), scatter_dimension=0, tiled=True),
    )
    inner_grads = (
        lax.psum_scatter(
            grad_query.astype(jnp.bfloat16), "dp", scatter_dimension=0, tiled=True
        ).astype(jnp.float32),
        lax.psum_scatter(
            grad_key.astype(jnp.bfloat16), "dp", scatter_dimension=0, tiled=True
        ).astype(jnp.float32),
        lax.psum_scatter(
            grad_value.astype(jnp.bfloat16), "dp", scatter_dimension=0, tiled=True
        ).astype(jnp.float32),
        lax.psum_scatter(
            grad_up.astype(jnp.bfloat16), "dp", scatter_dimension=0, tiled=True
        ).astype(jnp.float32),
    )
    outer_grads = (
        lax.psum_scatter(
            grad_out_proj.astype(jnp.bfloat16), "dp", scatter_dimension=1, tiled=True
        ).astype(jnp.float32),
        lax.psum_scatter(
            grad_down.astype(jnp.bfloat16), "dp", scatter_dimension=1, tiled=True
        ).astype(jnp.float32),
    )
    return (
        out_tokens,
        grad_tokens,
        gain_grads[0],
        inner_grads[0],
        inner_grads[1],
        inner_grads[2],
        outer_grads[0],
        gain_grads[1],
        inner_grads[3],
        outer_grads[1],
        jnp.sqrt(squares[0] / counted),
        jnp.sqrt(squares[1] / counted),
        jnp.sqrt(squares[2] / counted),
    )


def solution(mesh):
    placed = (
        P(("dp", "mp"), None),
        P("dp"),
        P(),
        P(),
        P(None, "mp"),
        P(None, "mp"),
        P(None, "mp"),
        P("mp", None),
        P(),
        P(None, "mp"),
        P("mp", None),
        P(("dp", "mp"), None),
    )
    return jax.shard_map(
        on_device,
        mesh=mesh,
        in_specs=placed,
        out_specs=(
            P(("dp", "mp"), None),
            P(("dp", "mp"), None),
            P(("dp", "mp")),
            P("dp", "mp"),
            P("dp", "mp"),
            P("dp", "mp"),
            P("mp", "dp"),
            P(("dp", "mp")),
            P("dp", "mp"),
            P("mp", "dp"),
            P(),
            P(),
            P(),
        ),
        check_vma=False,
    )
```

profile of v0, /device:TPU:0, one launch (start us, length us, event | category | flops | bytes accessed | tf_op | source)
XLA Modules:
  0.0 1085.7 jit_solution(5463557942506468040)
XLA Ops:
  8.8 58.3 %all-gather.3.cloned.1.call-done = bf16[2048,2048]{1,0:T(8,128)(2,1)} async-done(((bf16[256,2048]{1,0:T(8,128)(2,1)}), bf16[2048,2048]{1,0:T(8,128)(2,1)}) %all-gather.3.cloned.1.call-update) | async-done | bytes 8388624 | tf_op jit(solution)/shard_map/all_gather | solution.py:168
  72.2 8.7 fusion.28
  80.9 6.9 convolution_convert_fusion.8
  99.9 67.6 %while.27 = (s32[]{:T(128)}, bf16[4,512,256]{2,1,0:T(8,128)(2,1)}, f32[4,2,512]{2,1,0:T(2,128)S(1)}, s32[4]{0:T(128)S(1)}, s32[2048]{0:T(1024)S(1)}, /*index=5*/...) while((s32[]{:T(128)}, bf16[4,512,256]{2,1,0:T(8,128)(2,1)}, ...), condition=%wide.region_4.5_spmd, body=%wide.region_1.4_spmd.sunk | while | flops 1105331712 | bytes 37812440 | solution.py:79
  167.5 7.2 convolution_convert_fusion.2
  174.8 14.7 %fusion.62 = f32[2048,1024]{1,0:T(8,128)} fusion(bf16[2048,2048]{1,0:T(8,128)(2,1)} %all-gather.5.cloned.1.call-done, bf16[1024,2048]{1,0:T(8,128)(2,1)} %param.26), kind=kOutput, calls=%fused_computation.115 | convolution fusion | flops 8589934592 | bytes 20971520 | tf_op jit(solution)/shard_map/dot_general | solution.py:36
  189.5 112.2 %all-reduce.6.cloned.1.call-done = bf16[2048,2048]{1,0:T(8,128)(2,1)} async-done(((bf16[2048,2048]{1,0:T(8,128)(2,1)}), bf16[2048,2048]{1,0:T(8,128)(2,1)}) %all-reduce.6.cloned.1.call-update) | async-done | bytes 8388624 | tf_op jit(solution)/shard_map/psum | solution.py:176
  301.7 13.7 %convert_add_fusion = (f32[2048,2048]{1,0:T(8,128)}, f32[2048]{0:T(1024)S(1)}) fusion(bf16[2048,2048]{1,0:T(8,128)(2,1)} %all-gather.3.cloned.1.call-done, bf16[2048,2048]{1,0:T(8,128)(2,1)} %all-reduce.6.cloned.1.call-done), kind=kLoop, calls=%fused_computation.44 | loop fusion | flops 20969472 | bytes 33562624 | tf_op jit(solution)/shard_map/add | solution.py:179
  315.4 10.7 broadcast_multiply_fusion
  326.1 20.0 %fusion.35 = (bf16[2048,1024]{1,0:T(8,128)(2,1)S(1)}, f32[2048,1024]{1,0:T(8,128)}) fusion(f32[2048,1024]{1,0:T(8,128)} %fusion.62, bf16[2048,1024]{1,0:T(8,128)(2,1)S(1)} %copy-done.27, f32[2048,2048]{1,0:T(8,128)} %broadcast_multiply_fusion, f32[2048]{0:T(1024)S(1)} %copy-done.25), kind=kOutput, calls=%fused_computation.63 | convolution fusion | flops 8640266240 | bytes 41951232 | tf_op jit(solution)/shard_map/dot_general | solution.py:183
  348.0 11.3 %convolution_convert_fusion = bf16[2048,2048]{1,0:T(8,128)(2,1)} fusion(bf16[2048,1024]{1,0:T(8,128)(2,1)S(1)} %get-tuple-element.291, bf16[2048,1024]{1,0:T(8,128)(2,1)S(1)} %copy-done.27), kind=kOutput, calls=%fused_computation.66 | convolution fusion | flops 8594128896 | bytes 16777216 | tf_op jit(solution)/shard_map/dot_general | solution.py:36
  361.7 124.6 %all-reduce.8.cloned.1.call-done = bf16[2048,2048]{1,0:T(8,128)(2,1)} async-done(((bf16[2048,2048]{1,0:T(8,128)(2,1)}), bf16[2048,2048]{1,0:T(8,128)(2,1)}) %all-reduce.8.cloned.1.call-update) | async-done | bytes 8388624 | tf_op jit(solution)/shard_map/psum | solution.py:208
  486.3 9.2 multiply_reduce_fusion.1
  495.5 12.6 %multiply_add_fusion = f32[2048,2048]{1,0:T(8,128)S(1)} fusion(f32[2048,2048]{1,0:T(8,128)} %broadcast_multiply_fusion, bf16[2048,2048]{1,0:T(8,128)(2,1)} %all-gather.5.cloned.1.call-done, f32[2048]{0:T(1024)S(1)} %broadcast_multiply_fusion.1, bf16[2048,2048]{1,0:T(8,128)(2,1)} %all-reduce.8.cloned.1.call-done, f32[2048]{0:T(1024)S(1)} %copy-done.25, ...), kind=kLoop, calls=%fused_computation.51 | loop fusion | flops 29360128 | bytes 50356224 | tf_op jit(solution)/shard_map/add | solution.py:212
  517.1 9.1 fusion.43
  526.3 100.4 %while.28 = (s32[]{:T(128)}, f32[2048,2,128]{0,2,1:T(8,128)S(1)}, f32[2048,2,128]{0,2,1:T(8,128)}, bf16[4,512,256]{2,1,0:T(8,128)(2,1)}, s32[4]{0:T(128)S(1)}, /...) while((s32[]{:T(128)}, f32[2048,2,128]{0,2,1:T(8,128)S(1)}, ...), condition=%wide.region_13.14_spmd.clone, body=%wide.region_11.13_spmd.clone.sunk | while | flops 2724988416 | bytes 107800928 | solution.py:134
  626.8 7.1 convolution_convert_fusion.7
  634.1 6.9 convolution_convert_fusion.6
  642.8 6.9 convolution_convert_fusion.5
  649.8 15.4 %convolution_convert_fusion.4 = bf16[2048,1024]{1,0:T(8,128)(2,1)} fusion(bf16[2048,1024]{1,0:T(8,128)(2,1)} %copy-done.28, f32[2048,2048]{1,0:T(8,128)} %broadcast_multiply_fusion, f32[2048]{0:T(1024)S(1)} %copy-done.26), kind=kOutput, calls=%fused_computation.74 | convolution fusion | flops 8600420352 | bytes 25174016 | tf_op jit(solution)/shard_map/dot_general | solution.py:30
  665.3 16.3 %convolution_convert_fusion.3 = bf16[1024,2048]{1,0:T(8,128)(2,1)} fusion(bf16[2048,2048]{1,0:T(8,128)(2,1)} %all-gather.5.cloned.1.call-done, f32[2048,1024]{1,0:T(8,128)} %get-tuple-element.292), kind=kOutput, calls=%fused_computation.73 | convolution fusion | flops 8610906112 | bytes 20971520 | tf_op jit(solution)/shard_map/dot_general | solution.py:30
  681.6 15.7 %convolution_convert_fusion.1 = bf16[2048,2048]{1,0:T(8,128)(2,1)} fusion(bf16[1024,2048]{1,0:T(8,128)(2,1)} %param.26, f32[2048,1024]{1,0:T(8,128)} %get-tuple-element.292), kind=kOutput, calls=%fused_computation.67 | convolution fusion | flops 8613003264 | bytes 20971520 | tf_op jit(solution)/shard_map/dot_general | solution.py:186
  698.5 8.2 fusion.64
  706.8 8.1 fusion.63
  714.8 16.4 %add_convert_fusion = bf16[2048,2048]{1,0:T(8,128)(2,1)} fusion(f32[2048,2048]{1,0:T(8,128)} %fusion.63, f32[2048,2048]{1,0:T(8,128)} %fusion.64, bf16[2048,256]{0,1:T(8,128)(2,1)S(1)} %bitcast.131, bf16[2048,256]{1,0:T(8,128)(2,1)S(1)} %copy-done.19), kind=kOutput, calls=%fused_computation.50 | convolution fusion | flops 2160066560 | bytes 44040192 | tf_op jit(solution)/shard_map/dot_general | solution.py:36
  733.7 11.3 %convert_element_type.148 = f32[2048,2048]{1,0:T(8,128)} convert(bf16[2048,2048]{1,0:T(8,128)(2,1)} %all-reduce.6.cloned.1.call-done) | non-fusion elementwise | flops 4194304 | bytes 25165824 | tf_op jit(solution)/shard_map/convert_element_type | solution.py:178
  745.0 11.4 %convert_element_type.157 = f32[2048,2048]{1,0:T(8,128)} convert(bf16[2048,2048]{1,0:T(8,128)(2,1)} %all-reduce.8.cloned.1.call-done) | non-fusion elementwise | flops 4194304 | bytes 25165824 | tf_op jit(solution)/shard_map/convert_element_type | solution.py:208
  766.1 30.6 %reduce-scatter.21.cloned.1.call-done = bf16[512,1024]{1,0:T(8,128)(2,1)} async-done(((bf16[2048,1024]{1,0:T(8,128)(2,1)}), bf16[512,1024]{1,0:T(8,128)(2,1)}) %reduce-scatter.21.cloned.1.call-update) | async-done | bytes 1048592 | tf_op jit(solution)/shard_map/reduce_scatter | solution.py:251
  799.5 76.7 %reduce-scatter.23.cloned.1.call-done = bf16[1024,512]{1,0:T(8,128)(2,1)} async-done(((bf16[1024,2048]{1,0:T(8,128)(2,1)}), bf16[1024,512]{1,0:T(8,128)(2,1)}) %reduce-scatter.23.cloned.1.call-update) | async-done | bytes 1048592 | tf_op jit(solution)/shard_map/reduce_scatter | solution.py:259
  879.0 72.4 %reduce-scatter.9.cloned.1.call-done = bf16[256,2048]{1,0:T(8,128)(2,1)} async-done(((bf16[2048,2048]{1,0:T(8,128)(2,1)}), bf16[256,2048]{1,0:T(8,128)(2,1)}) %reduce-scatter.9.cloned.1.call-update) | async-done | bytes 1048592 | tf_op jit(solution)/shard_map/reduce_scatter | solution.py:185
  956.4 70.1 %reduce-scatter.11.cloned.1.call-done = bf16[256,2048]{1,0:T(8,128)(2,1)} async-done(((bf16[2048,2048]{1,0:T(8,128)(2,1)}), bf16[256,2048]{1,0:T(8,128)(2,1)}) %reduce-scatter.11.cloned.1.call-update) | async-done | bytes 1048592 | tf_op jit(solution)/shard_map/reduce_scatter | solution.py:228
  1028.5 39.9 %all-reduce.2 = (f32[2048]{0:T(1024)S(1)}, f32[2048]{0:T(1024)S(1)}, f32[]{:T(128)}, f32[]{:T(128)}, f32[]{:T(128)}) all-reduce(f32[2048]{0:T(1024)S(1)} %get-tuple-element.232, f32[2048]{0:T(1024)S(1)} %fusion.59, f32[]{:T(128)} %get-tuple-element.235, f32[]{:T(128)} %get-tuple-element.236, ...), channel_id=4, replica_groups=mesh['dp'=4,'mp'=8] {'dp','mp'}, use_global_device_ids=true, to_apply=%region_17.18.clone | all-reduce | flops 4099 | bytes 32792
  (270 shorter events, 215.5 us)
Async XLA Ops:
  7.2 160.3 %copy-start = (bf16[256,2048]{1,0:T(8,128)(2,1)S(1)}, bf16[256,2048]{1,0:T(8,128)(2,1)}, u32[]{:S(2)}) copy-start(bf16[256,2048]{1,0:T(8,128)(2,1)} %param.23) | copy-start | bytes 3145732
  7.2 65.0 %copy-start.23 = (f32[2048]{0:T(1024)S(1)}, f32[2048]{0:T(1024)}, u32[]{:S(2)}) copy-start(f32[2048]{0:T(1024)} %param.19) | copy-start | bytes 24580
  7.2 59.8 %all-gather.3.cloned.1.call-start = ((), (), s32[]{:S(2)}) async-start(), calls=%async_computation.8 | async-start | bytes 9437184 | tf_op jit(solution)/shard_map/all_gather | solution.py:168
  7.9 166.9 %all-gather.5.cloned.1.call-start = ((), (), s32[]{:S(2)}) async-start(), calls=%async_computation.11 | async-start | bytes 9437184 | tf_op jit(solution)/shard_map/all_gather | solution.py:203
  8.7 293.0 %all-reduce.6.cloned.1.call-start = ((), (), s32[]{:S(2)}) async-start(), calls=%async_computation.9 | async-start | bytes 16777216 | tf_op jit(solution)/shard_map/psum | solution.py:176
  72.2 8.7 copy-start.18
  90.2 8.2 copy-start.4
  91.7 8.2 copy-start.13
  91.7 8.2 dynamic-slice-start
  167.5 7.3 copy-start.8
  174.7 311.5 %all-reduce.8.cloned.1.call-start = ((), (), s32[]{:S(2)}) async-start(), calls=%async_computation.12 | async-start | bytes 16777216 | tf_op jit(solution)/shard_map/psum | solution.py:208
  301.7 13.7 %copy-start.3 = (bf16[2048,2048]{1,0:T(8,128)(2,1)S(1)}, bf16[2048,2048]{1,0:T(8,128)(2,1)}, u32[]{:S(2)}) copy-start(bf16[2048,2048]{1,0:T(8,128)(2,1)} %all-reduce.6.cloned.1.call-done) | copy-start | bytes 25165828
  315.4 10.7 copy-start.25
  315.4 10.7 copy-start.27
  359.4 399.5 %reduce-scatter.19.cloned.1.call-start = ((), (), s32[]{:S(2)}) async-start(), calls=%async_computation.17 | async-start | bytes 1310720 | tf_op jit(solution)/shard_map/reduce_scatter | solution.py:256
  495.5 18.3 %copy-start.10 = (bf16[4,512,256]{2,1,0:T(8,128)(2,1)S(1)}, bf16[4,512,256]{2,1,0:T(8,128)(2,1)}, u32[]{:S(2)}) copy-start(bf16[4,512,256]{2,1,0:T(8,128)(2,1)} %get-tuple-element.125) | copy-start | bytes 3145732
  526.3 234.4 %reduce-scatter.13.cloned.1.call-start = ((), (), s32[]{:S(2)}) async-start(), calls=%async_computation.14 | async-start | bytes 1310720 | tf_op jit(solution)/shard_map/reduce_scatter | solution.py:242
  531.0 7.5 copy-start.11
  556.0 7.5 copy-start.11
  581.0 7.5 copy-start.11
  606.0 7.5 copy-start.11
  633.9 128.6 %reduce-scatter.15.cloned.1.call-start = ((), (), s32[]{:S(2)}) async-start(), calls=%async_computation.15 | async-start | bytes 1310720 | tf_op jit(solution)/shard_map/reduce_scatter | solution.py:245
  641.0 123.3 %reduce-scatter.17.cloned.1.call-start = ((), (), s32[]{:S(2)}) async-start(), calls=%async_computation.16 | async-start | bytes 1310720 | tf_op jit(solution)/shard_map/reduce_scatter | solution.py:248
  649.7 146.9 %reduce-scatter.21.cloned.1.call-start = ((), (), s32[]{:S(2)}) async-start(), calls=%async_computation.18 | async-start | bytes 5242880 | tf_op jit(solution)/shard_map/reduce_scatter | solution.py:251
  665.2 210.9 %reduce-scatter.23.cloned.1.call-start = ((), (), s32[]{:S(2)}) async-start(), calls=%async_computation.19 | async-start | bytes 5242880 | tf_op jit(solution)/shard_map/reduce_scatter | solution.py:259
  681.6 269.8 %reduce-scatter.9.cloned.1.call-start = ((), (), s32[]{:S(2)}) async-start(), calls=%async_computation.10 | async-start | bytes 9437184 | tf_op jit(solution)/shard_map/reduce_scatter | solution.py:185
  697.3 329.1 %reduce-scatter.11.cloned.1.call-start = ((), (), s32[]{:S(2)}) async-start(), calls=%async_computation.13 | async-start | bytes 9437184 | tf_op jit(solution)/shard_map/reduce_scatter | solution.py:228
  698.5 8.2 copy-start.17
  698.5 8.2 copy-start.20
  706.8 8.1 copy-start.19
  758.9 267.6 %copy-start.24 = (f32[2048]{0:T(1024)S(1)}, f32[2048]{0:T(1024)}, u32[]{:S(2)}) copy-start(f32[2048]{0:T(1024)} %param.19) | copy-start | bytes 24580
  796.6 278.6 %copy-start.1 = (bf16[256,2048]{1,0:T(8,128)(2,1)S(1)}, bf16[256,2048]{1,0:T(8,128)(2,1)}, u32[]{:S(2)}) copy-start(bf16[256,2048]{1,0:T(8,128)(2,1)} %param.23) | copy-start | bytes 3145732
  (25 other events, 98.7 us)
Sparse Core Ops, SparseCore 0:
  9.9 57.0 all-gather.2
  68.9 54.3 all-gather.4
  174.9 126.7 all-reduce.5
  359.5 126.7 all-reduce.7
  526.4 27.3 reduce-scatter.18
  634.0 27.3 reduce-scatter.12
  664.2 25.7 reduce-scatter.14
  693.0 25.7 reduce-scatter.16
  721.2 75.4 reduce-scatter.20
  798.9 77.2 reduce-scatter.22
  879.6 71.7 reduce-scatter.8
  955.1 71.2 reduce-scatter.10
where the time goes:
time: 1090 us
  waiting for transfers between devices  546 us (50%)
  matrix products  256 us (23%)
  other arithmetic  167 us (15%)
  blocking collectives  39.9 us (4%)
  local copies, waits for them, and re-layouts  38.6 us (4%)
  between operations  20.9 us (2%)
  loops' own time  16.8 us (2%)
    psum x1, waiting for transfers between devices, on_device(): lax.psum(contract_cols(grad_pre, w_up).astype(jnp.bfloat16), 'mp')  125 us
    psum x1, waiting for transfers between devices, on_device(): lax.psum(jnp.dot(mixed, w_out, preferred_element_type=jnp.float32).astype...  112 us
    reduce_scatter x1, waiting for transfers between devices, on_device(): lax.psum_scatter(grad_down.astype(jnp.bfloat16), 'dp', scatter_dimension=...  76.7 us
    reduce_scatter x1, waiting for transfers between devices, on_device(): lax.psum_scatter(jnp.dot(hidden, w_down, preferred_element_type=jnp.float...  72.4 us
    reduce_scatter x1, waiting for transfers between devices, on_device(): lax.psum_scatter((total_term + contract_cols(grad_values, w_value)).astyp...  70.1 us
    dot_general x6, matrix products, contract_cols(): lax.dot_general(left_side, right_side, (((1,), (1,)), ((), ())), preferre...  67.8 us
    all_gather x1, waiting for transfers between devices, on_device(): gathered = lax.all_gather(tokens, 'mp', axis=0, tiled=True)  58.3 us
    dot_general x6, matrix products, contract_rows(): lax.dot_general(left_side, right_side, (((0,), (0,)), ((), ())), preferre...  55.9 us
  transfers between devices with their start and end apart: 12, of which 7 were waited for; matrix products, arithmetic and copies ran while one was open for 33% of the time, Pallas kernels for 0%

commit v1 on v0

--- a/solution.py
+++ b/solution.py
@@ -165,7 +165,33 @@
     valid_group = lax.dynamic_slice_in_dim(valid, dp_index * seq_rows, seq_rows)
     valid_own = lax.dynamic_slice_in_dim(valid_group, own_first, own_rows)
     token_values = tokens.astype(jnp.float32)
-    gathered = lax.all_gather(tokens, "mp", axis=0, tiled=True)
+    kept_rows = []
+    b = 0
+    z1, built, p_next = (lax.axis_size("mp"), lax.axis_index("mp"), tokens.shape[0])
+    while b < z1:
+        kept_rows.append((b, (b + 1) % z1))
+        b = b + 1
+    found = []
+    b = 0
+    while b < z1:
+        found.append((b, (b - 1) % z1))
+        b = b + 1
+    gathered = jnp.zeros((*tokens.shape[:0], z1 * p_next, *tokens.shape[1:]), tokens.dtype)
+    gathered = lax.dynamic_update_slice_in_dim(gathered, tokens, built * p_next, axis=0)
+    answer = z1 // 2
+    jj = 1
+    view_out = formed = tokens
+    while jj < answer + 1:
+        view_out = lax.ppermute(view_out, axis_name="mp", perm=kept_rows)
+        gathered = lax.dynamic_update_slice_in_dim(
+            gathered, view_out, (built - jj) % z1 * p_next, axis=0
+        )
+        if jj < z1 - answer:
+            formed = lax.ppermute(formed, axis_name="mp", perm=found)
+            gathered = lax.dynamic_update_slice_in_dim(
+                gathered, formed, (built + jj) % z1 * p_next, axis=0
+            )
+        jj += 1
     normed_attn = norm_rows(gathered.astype(jnp.float32), gain_attn).astype(jnp.bfloat16)
     queries = jnp.dot(normed_attn, w_query, preferred_element_type=jnp.float32).astype(jnp.bfloat16)
     keys_all = jnp.dot(normed_attn, w_key, preferred_element_type=jnp.float32).astype(jnp.bfloat16)

time: 1090 us -> 1180 us (1.083)
  waiting for transfers between devices: 546 us -> 612 us
    ppermute x0 -> x7, waiting for transfers between devices: none -> 72.9 us  [the longest x4 71.2 us: on_device(): view_out = lax.ppermute(view_out, axis_name='mp', perm=kept_rows)]
    all_gather x1 -> x0, waiting for transfers between devices: 58.3 us -> none  [on_device(): gathered = lax.all_gather(tokens, 'mp', axis=0, tiled=True)]
    all_gather x1, waiting for transfers between devices: 0.02 us -> 31.5 us  [on_device(): grad_rows = lax.all_gather(grad_out, 'mp', axis=0, tiled=True)]
    psum x1, waiting for transfers between devices: 112 us -> 133 us  [on_device(): lax.psum(jnp.dot(mixed, w_out, preferred_element_type=jnp.float32).astype...]
  transfers between devices with their start and end apart: 12 -> 18, of which waited for: 7 -> 13; matrix products, arithmetic and copies ran while one was open for 33% -> 23% of each run, Pallas kernels for 0% -> 0%
where the time goes in v1:
time: 1180 us; the launch traced here: 1170 us
  waiting for transfers between devices  612 us (52%)
  matrix products  255 us (22%)
  other arithmetic  164 us (14%)
  local copies, waits for them, and re-layouts  47.6 us (4%)
  blocking collectives  39.9 us (3%)
  between operations  20.8 us (2%)
  loops' own time  17.1 us (1%)
    psum x1, waiting for transfers between devices, on_device(): lax.psum(jnp.dot(mixed, w_out, preferred_element_type=jnp.float32).astype...  133 us
    psum x1, waiting for transfers between devices, on_device(): lax.psum(contract_cols(grad_pre, w_up).astype(jnp.bfloat16), 'mp')  124 us
    reduce_scatter x1, waiting for transfers between devices, on_device(): lax.psum_scatter(grad_down.astype(jnp.bfloat16), 'dp', scatter_dimension=...  76.8 us
    reduce_scatter x1, waiting for transfers between devices, on_device(): lax.psum_scatter(jnp.dot(hidden, w_down, preferred_element_type=jnp.float...  72.3 us
    ppermute x4, waiting for transfers between devices, on_device(): view_out = lax.ppermute(view_out, axis_name='mp', perm=kept_rows)  71.2 us
    reduce_scatter x1, waiting for transfers between devices, on_device(): lax.psum_scatter((total_term + contract_cols(grad_values, w_value)).astyp...  70.2 us
    dot_general x6, matrix products, contract_cols(): lax.dot_general(left_side, right_side, (((1,), (1,)), ((), ())), preferre...  67.7 us
    dot_general x6, matrix products, contract_rows(): lax.dot_general(left_side, right_side, (((0,), (0,)), ((), ())), preferre...  55.8 us
  transfers between devices with their start and end apart: 18, of which 13 were waited for; matrix products, arithmetic and copies ran while one was open for 23% of the time, Pallas kernels for 0%

profile of v1, /device:TPU:0, one launch (start us, length us, event | category | flops | bytes accessed | tf_op | source)
XLA Modules:
  0.0 1167.3 jit_solution(8582457588591752917)
XLA Ops:
  10.7 21.2 %collective-permute-done = bf16[256,2048]{1,0:T(8,128)(2,1)S(1)} collective-permute-done((bf16[256,2048]{1,0:T(8,128)(2,1)}, bf16[256,2048]{1,0:T(8,128)(2,1)S(1)}, u32[]{:S(2)}, u32[]{:S(2)}) %collective-permute-start) | collective-permute-done | bytes 1048608 | tf_op jit(solution)/shard_map/ppermute | solution.py:185
  36.2 19.5 %collective-permute-done.2 = bf16[256,2048]{1,0:T(8,128)(2,1)} collective-permute-done((bf16[256,2048]{1,0:T(8,128)(2,1)S(1)}, bf16[256,2048]{1,0:T(8,128)(2,1)}, u32[]{:S(2)}, u32[]{:S(2)}) %collective-permute-start.2) | collective-permute-done | bytes 1048608 | tf_op jit(solution)/shard_map/ppermute | solution.py:185
  60.9 19.4 %collective-permute-done.4 = bf16[256,2048]{1,0:T(8,128)(2,1)} collective-permute-done((bf16[256,2048]{1,0:T(8,128)(2,1)}, bf16[256,2048]{1,0:T(8,128)(2,1)}, u32[]{:S(2)}, u32[]{:S(2)}) %collective-permute-start.4) | collective-permute-done | bytes 1048608 | tf_op jit(solution)/shard_map/ppermute | solution.py:185
  84.6 11.1 collective-permute-done.6
  100.7 8.7 fusion.28
  128.5 67.6 %while.27 = (s32[]{:T(128)}, bf16[4,512,256]{2,1,0:T(8,128)(2,1)}, f32[4,2,512]{2,1,0:T(2,128)S(1)}, s32[4]{0:T(128)S(1)}, s32[2048]{0:T(1024)S(1)}, /*index=5*/...) while((s32[]{:T(128)}, bf16[4,512,256]{2,1,0:T(8,128)(2,1)}, ...), condition=%wide.region_4.5_spmd, body=%wide.region_1.4_spmd.sunk | while | flops 1105331712 | bytes 37812440 | solution.py:79
  196.0 7.2 convolution_convert_fusion.2
  204.0 132.5 %all-reduce.6.cloned.1.call-done = bf16[2048,2048]{1,0:T(8,128)(2,1)} async-done(((bf16[2048,2048]{1,0:T(8,128)(2,1)}), bf16[2048,2048]{1,0:T(8,128)(2,1)}) %all-reduce.6.cloned.1.call-update) | async-done | bytes 8388624 | tf_op jit(solution)/shard_map/psum | solution.py:202
  336.6 14.7 %convert_add_fusion = (f32[2048,2048]{1,0:T(8,128)}, f32[2048]{0:T(1024)S(1)}) fusion(bf16[2048,2048]{1,0:T(8,128)(2,1)} %copy-done.3, bf16[2048,2048]{1,0:T(8,128)(2,1)} %all-reduce.6.cloned.1.call-done), kind=kLoop, calls=%fused_computation.44 | loop fusion | flops 20969472 | bytes 33562624 | tf_op jit(solution)/shard_map/add | solution.py:205
  351.3 10.4 broadcast_multiply_fusion
  361.7 31.5 %all-gather.2.cloned.1.call-done = bf16[2048,2048]{1,0:T(8,128)(2,1)} async-done(((bf16[256,2048]{1,0:T(8,128)(2,1)}), bf16[2048,2048]{1,0:T(8,128)(2,1)}) %all-gather.2.cloned.1.call-update) | async-done | bytes 8388624 | tf_op jit(solution)/shard_map/all_gather | solution.py:229
  393.2 14.6 %fusion.62 = f32[2048,1024]{1,0:T(8,128)} fusion(bf16[2048,2048]{1,0:T(8,128)(2,1)} %all-gather.2.cloned.1.call-done, bf16[1024,2048]{1,0:T(8,128)(2,1)} %param.26), kind=kOutput, calls=%fused_computation.123 | convolution fusion | flops 8589934592 | bytes 20971520 | tf_op jit(solution)/shard_map/dot_general | solution.py:36
  407.8 20.1 %fusion.35 = (bf16[2048,1024]{1,0:T(8,128)(2,1)S(1)}, f32[2048,1024]{1,0:T(8,128)}) fusion(f32[2048,1024]{1,0:T(8,128)} %fusion.62, bf16[2048,1024]{1,0:T(8,128)(2,1)S(1)} %copy-done.31, f32[2048,2048]{1,0:T(8,128)} %broadcast_multiply_fusion, f32[2048]{0:T(1024)S(1)} %copy-done.29), kind=kOutput, calls=%fused_computation.63 | convolution fusion | flops 8640266240 | bytes 41951232 | tf_op jit(solution)/shard_map/dot_general | solution.py:209
  429.9 11.1 convolution_convert_fusion
  443.4 124.4 %all-reduce.8.cloned.1.call-done = bf16[2048,2048]{1,0:T(8,128)(2,1)} async-done(((bf16[2048,2048]{1,0:T(8,128)(2,1)}), bf16[2048,2048]{1,0:T(8,128)(2,1)}) %all-reduce.8.cloned.1.call-update) | async-done | bytes 8388624 | tf_op jit(solution)/shard_map/psum | solution.py:234
  567.8 9.2 multiply_reduce_fusion.1
  577.0 12.6 %multiply_add_fusion = f32[2048,2048]{1,0:T(8,128)S(1)} fusion(f32[2048,2048]{1,0:T(8,128)} %broadcast_multiply_fusion, bf16[2048,2048]{1,0:T(8,128)(2,1)} %all-gather.2.cloned.1.call-done, f32[2048]{0:T(1024)S(1)} %broadcast_multiply_fusion.1, bf16[2048,2048]{1,0:T(8,128)(2,1)} %all-reduce.8.cloned.1.call-done, f32[2048]{0:T(1024)S(1)} %copy-done.29, ...), kind=kLoop, calls=%fused_computation.51 | loop fusion | flops 29360128 | bytes 50356224 | tf_op jit(solution)/shard_map/add | solution.py:238
  598.6 9.1 fusion.43
  607.8 100.7 %while.28 = (s32[]{:T(128)}, f32[2048,2,128]{0,2,1:T(8,128)S(1)}, f32[2048,2,128]{0,2,1:T(8,128)}, bf16[4,512,256]{2,1,0:T(8,128)(2,1)}, s32[4]{0:T(128)S(1)}, /...) while((s32[]{:T(128)}, f32[2048,2,128]{0,2,1:T(8,128)S(1)}, ...), condition=%wide.region_13.14_spmd.clone, body=%wide.region_11.13_spmd.clone.sunk | while | flops 2724988416 | bytes 107800928 | solution.py:134
  731.5 15.3 %convolution_convert_fusion.4 = bf16[2048,1024]{1,0:T(8,128)(2,1)} fusion(bf16[2048,1024]{1,0:T(8,128)(2,1)} %copy-done.32, f32[2048,2048]{1,0:T(8,128)} %broadcast_multiply_fusion, f32[2048]{0:T(1024)S(1)} %copy-done.30), kind=kOutput, calls=%fused_computation.74 | convolution fusion | flops 8600420352 | bytes 25174016 | tf_op jit(solution)/shard_map/dot_general | solution.py:30
  746.9 16.3 %convolution_convert_fusion.3 = bf16[1024,2048]{1,0:T(8,128)(2,1)} fusion(bf16[2048,2048]{1,0:T(8,128)(2,1)} %all-gather.2.cloned.1.call-done, f32[2048,1024]{1,0:T(8,128)} %get-tuple-element.292), kind=kOutput, calls=%fused_computation.73 | convolution fusion | flops 8610906112 | bytes 20971520 | tf_op jit(solution)/shard_map/dot_general | solution.py:30
  763.3 15.4 %convolution_convert_fusion.1 = bf16[2048,2048]{1,0:T(8,128)(2,1)} fusion(bf16[1024,2048]{1,0:T(8,128)(2,1)} %param.26, f32[2048,1024]{1,0:T(8,128)} %get-tuple-element.292), kind=kOutput, calls=%fused_computation.67 | convolution fusion | flops 8613003264 | bytes 20971520 | tf_op jit(solution)/shard_map/dot_general | solution.py:212
  780.0 8.2 fusion.64
  788.2 8.1 fusion.63
  796.3 16.5 %add_convert_fusion = bf16[2048,2048]{1,0:T(8,128)(2,1)} fusion(f32[2048,2048]{1,0:T(8,128)} %fusion.63, f32[2048,2048]{1,0:T(8,128)} %fusion.64, bf16[2048,256]{0,1:T(8,128)(2,1)S(1)} %bitcast.131, bf16[2048,256]{1,0:T(8,128)(2,1)S(1)} %copy-done.21), kind=kOutput, calls=%fused_computation.50 | convolution fusion | flops 2160066560 | bytes 44040192 | tf_op jit(solution)/shard_map/dot_general | solution.py:36
  815.2 11.3 convert_element_type.148
  826.6 11.4 convert_element_type.157
  847.6 30.6 %reduce-scatter.21.cloned.1.call-done = bf16[512,1024]{1,0:T(8,128)(2,1)} async-done(((bf16[2048,1024]{1,0:T(8,128)(2,1)}), bf16[512,1024]{1,0:T(8,128)(2,1)}) %reduce-scatter.21.cloned.1.call-update) | async-done | bytes 1048592 | tf_op jit(solution)/shard_map/reduce_scatter | solution.py:277
  881.1 76.8 %reduce-scatter.23.cloned.1.call-done = bf16[1024,512]{1,0:T(8,128)(2,1)} async-done(((bf16[1024,2048]{1,0:T(8,128)(2,1)}), bf16[1024,512]{1,0:T(8,128)(2,1)}) %reduce-scatter.23.cloned.1.call-update) | async-done | bytes 1048592 | tf_op jit(solution)/shard_map/reduce_scatter | solution.py:285
  960.7 72.3 %reduce-scatter.9.cloned.1.call-done = bf16[256,2048]{1,0:T(8,128)(2,1)} async-done(((bf16[2048,2048]{1,0:T(8,128)(2,1)}), bf16[256,2048]{1,0:T(8,128)(2,1)}) %reduce-scatter.9.cloned.1.call-update) | async-done | bytes 1048592 | tf_op jit(solution)/shard_map/reduce_scatter | solution.py:211
  1038.0 70.2 %reduce-scatter.11.cloned.1.call-done = bf16[256,2048]{1,0:T(8,128)(2,1)} async-done(((bf16[2048,2048]{1,0:T(8,128)(2,1)}), bf16[256,2048]{1,0:T(8,128)(2,1)}) %reduce-scatter.11.cloned.1.call-update) | async-done | bytes 1048592 | tf_op jit(solution)/shard_map/reduce_scatter | solution.py:254
  1110.2 39.9 %all-reduce.2 = (f32[2048]{0:T(1024)S(1)}, f32[2048]{0:T(1024)S(1)}, f32[]{:T(128)}, f32[]{:T(128)}, f32[]{:T(128)}) all-reduce(f32[2048]{0:T(1024)S(1)} %get-tuple-element.232, f32[2048]{0:T(1024)S(1)} %fusion.59, f32[]{:T(128)} %get-tuple-element.235, f32[]{:T(128)} %get-tuple-element.236, ...), channel_id=4, replica_groups=mesh['dp'=4,'mp'=8] {'dp','mp'}, use_global_device_ids=true, to_apply=%region_17.18.clone | all-reduce | flops 4099 | bytes 32792
  (298 shorter events, 259.7 us)
Async XLA Ops:
  7.2 188.9 %copy-start = (bf16[256,2048]{1,0:T(8,128)(2,1)S(1)}, bf16[256,2048]{1,0:T(8,128)(2,1)}, u32[]{:S(2)}) copy-start(bf16[256,2048]{1,0:T(8,128)(2,1)} %param.23) | copy-start | bytes 3145732
  7.2 49.8 %copy-start.8 = (bf16[256,2048]{1,0:T(8,128)(2,1)S(1)}, bf16[256,2048]{1,0:T(8,128)(2,1)}, u32[]{:S(2)}) copy-start(bf16[256,2048]{1,0:T(8,128)(2,1)} %param.16) | copy-start | bytes 3145732
  7.2 329.3 %all-reduce.6.cloned.1.call-start = ((), (), s32[]{:S(2)}) async-start(), calls=%async_computation.8 | async-start | bytes 16777216 | tf_op jit(solution)/shard_map/psum | solution.py:202
  7.3 24.7 %collective-permute-start = (bf16[256,2048]{1,0:T(8,128)(2,1)}, bf16[256,2048]{1,0:T(8,128)(2,1)S(1)}, u32[]{:S(2)}, u32[]{:S(2)}) collective-permute-start(bf16[256,2048]{1,0:T(8,128)(2,1)} %param.16), channel_id=1, source_target_pairs={{0,1},{1,2},{2,3},{3,4},{4,5},{5,6},{6,7},{7,0},{8,9},{9,10},{10,1... | collective-permute-start | bytes 3145736 | tf_op jit(solution)/shard_map/ppermute | solution.py:185
  7.8 25.8 %collective-permute-start.1 = (bf16[256,2048]{1,0:T(8,128)(2,1)}, bf16[256,2048]{1,0:T(8,128)(2,1)S(1)}, u32[]{:S(2)}, u32[]{:S(2)}) collective-permute-start(bf16[256,2048]{1,0:T(8,128)(2,1)} %param.16), channel_id=1, source_target_pairs={{0,7},{1,0},{2,1},{3,2},{4,3},{5,4},{6,5},{7,6},{8,15},{9,8},{10,9... | collective-permute-start | bytes 3145736 | tf_op jit(solution)/shard_map/ppermute | solution.py:190
  31.9 23.8 %collective-permute-start.2 = (bf16[256,2048]{1,0:T(8,128)(2,1)S(1)}, bf16[256,2048]{1,0:T(8,128)(2,1)}, u32[]{:S(2)}, u32[]{:S(2)}) collective-permute-start(bf16[256,2048]{1,0:T(8,128)(2,1)S(1)} %collective-permute-done), channel_id=1, source_target_pairs={{0,1},{1,2},{2,3},{3,4},{4,5},{5,6},{6,7},{7,0},{8,9},{9,10},{10,1... | collective-permute-start | bytes 3145736 | tf_op jit(solution)/shard_map/ppermute | solution.py:185
  33.5 24.3 %collective-permute-start.3 = (bf16[256,2048]{1,0:T(8,128)(2,1)S(1)}, bf16[256,2048]{1,0:T(8,128)(2,1)}, u32[]{:S(2)}, u32[]{:S(2)}) collective-permute-start(bf16[256,2048]{1,0:T(8,128)(2,1)S(1)} %collective-permute-done.1), channel_id=1, source_target_pairs={{0,7},{1,0},{2,1},{3,2},{4,3},{5,4},{6,5},{7,6},{8,15},{9,8},{10,9... | collective-permute-start | bytes 3145736 | tf_op jit(solution)/shard_map/ppermute | solution.py:190
  55.7 24.6 %collective-permute-start.4 = (bf16[256,2048]{1,0:T(8,128)(2,1)}, bf16[256,2048]{1,0:T(8,128)(2,1)}, u32[]{:S(2)}, u32[]{:S(2)}) collective-permute-start(bf16[256,2048]{1,0:T(8,128)(2,1)} %collective-permute-done.2), channel_id=1, source_target_pairs={{0,1},{1,2},{2,3},{3,4},{4,5},{5,6},{6,7},{7,0},{8,9},{9,10},{10,1... | collective-permute-start | bytes 3145736 | tf_op jit(solution)/shard_map/ppermute | solution.py:185
  57.8 26.6 %collective-permute-start.5 = (bf16[256,2048]{1,0:T(8,128)(2,1)}, bf16[256,2048]{1,0:T(8,128)(2,1)S(1)}, u32[]{:S(2)}, u32[]{:S(2)}) collective-permute-start(bf16[256,2048]{1,0:T(8,128)(2,1)} %collective-permute-done.3), channel_id=1, source_target_pairs={{0,7},{1,0},{2,1},{3,2},{4,3},{5,4},{6,5},{7,6},{8,15},{9,8},{10,9... | collective-permute-start | bytes 3145736 | tf_op jit(solution)/shard_map/ppermute | solution.py:190
  80.3 15.3 %collective-permute-start.6 = (bf16[256,2048]{1,0:T(8,128)(2,1)}, bf16[256,2048]{1,0:T(8,128)(2,1)S(1)}, u32[]{:S(2)}, u32[]{:S(2)}) collective-permute-start(bf16[256,2048]{1,0:T(8,128)(2,1)} %collective-permute-done.4), channel_id=1, source_target_pairs={{0,1},{1,2},{2,3},{3,4},{4,5},{5,6},{6,7},{7,0},{8,9},{9,10},{10,1... | collective-permute-start | bytes 3145736 | tf_op jit(solution)/shard_map/ppermute | solution.py:185
  81.8 19.0 %copy-start.27 = (f32[2048]{0:T(1024)S(1)}, f32[2048]{0:T(1024)}, u32[]{:S(2)}) copy-start(f32[2048]{0:T(1024)} %param.19) | copy-start | bytes 24580
  100.7 8.7 copy-start.20
  118.7 8.3 copy-start.5
  120.2 8.2 dynamic-slice-start
  203.2 190.0 %all-gather.2.cloned.1.call-start = ((), (), s32[]{:S(2)}) async-start(), calls=%async_computation.10 | async-start | bytes 9437184 | tf_op jit(solution)/shard_map/all_gather | solution.py:229
  204.0 363.8 %all-reduce.8.cloned.1.call-start = ((), (), s32[]{:S(2)}) async-start(), calls=%async_computation.11 | async-start | bytes 16777216 | tf_op jit(solution)/shard_map/psum | solution.py:234
  336.6 14.7 %copy-start.4 = (bf16[2048,2048]{1,0:T(8,128)(2,1)S(1)}, bf16[2048,2048]{1,0:T(8,128)(2,1)}, u32[]{:S(2)}) copy-start(bf16[2048,2048]{1,0:T(8,128)(2,1)} %all-reduce.6.cloned.1.call-done) | copy-start | bytes 25165828
  361.7 46.2 %copy-start.29 = (f32[2048]{0:T(1024)S(1)}, f32[2048]{0:T(1024)}, u32[]{:S(2)}) copy-start(f32[2048]{0:T(1024)} %param.24) | copy-start | bytes 24580
  393.2 14.6 %copy-start.31 = (bf16[2048,1024]{1,0:T(8,128)(2,1)S(1)}, bf16[2048,1024]{1,0:T(8,128)(2,1)}, u32[]{:S(2)}) copy-start(bf16[2048,1024]{1,0:T(8,128)(2,1)} %param.25) | copy-start | bytes 12582916
  441.0 399.4 %reduce-scatter.19.cloned.1.call-start = ((), (), s32[]{:S(2)}) async-start(), calls=%async_computation.16 | async-start | bytes 1310720 | tf_op jit(solution)/shard_map/reduce_scatter | solution.py:282
  577.0 18.3 %copy-start.12 = (bf16[4,512,256]{2,1,0:T(8,128)(2,1)S(1)}, bf16[4,512,256]{2,1,0:T(8,128)(2,1)}, u32[]{:S(2)}) copy-start(bf16[4,512,256]{2,1,0:T(8,128)(2,1)} %get-tuple-element.125) | copy-start | bytes 3145732
  607.8 234.5 %reduce-scatter.13.cloned.1.call-start = ((), (), s32[]{:S(2)}) async-start(), calls=%async_computation.13 | async-start | bytes 1310720 | tf_op jit(solution)/shard_map/reduce_scatter | solution.py:268
  715.6 128.4 %reduce-scatter.15.cloned.1.call-start = ((), (), s32[]{:S(2)}) async-start(), calls=%async_computation.14 | async-start | bytes 1310720 | tf_op jit(solution)/shard_map/reduce_scatter | solution.py:271
  722.7 123.1 %reduce-scatter.17.cloned.1.call-start = ((), (), s32[]{:S(2)}) async-start(), calls=%async_computation.15 | async-start | bytes 1310720 | tf_op jit(solution)/shard_map/reduce_scatter | solution.py:274
  731.4 146.7 %reduce-scatter.21.cloned.1.call-start = ((), (), s32[]{:S(2)}) async-start(), calls=%async_computation.17 | async-start | bytes 5242880 | tf_op jit(solution)/shard_map/reduce_scatter | solution.py:277
  746.9 211.0 %reduce-scatter.23.cloned.1.call-start = ((), (), s32[]{:S(2)}) async-start(), calls=%async_computation.18 | async-start | bytes 5242880 | tf_op jit(solution)/shard_map/reduce_scatter | solution.py:285
  763.2 269.8 %reduce-scatter.9.cloned.1.call-start = ((), (), s32[]{:S(2)}) async-start(), calls=%async_computation.9 | async-start | bytes 9437184 | tf_op jit(solution)/shard_map/reduce_scatter | solution.py:211
  778.7 329.5 %reduce-scatter.11.cloned.1.call-start = ((), (), s32[]{:S(2)}) async-start(), calls=%async_computation.12 | async-start | bytes 9437184 | tf_op jit(solution)/shard_map/reduce_scatter | solution.py:254
  780.0 8.2 copy-start.19
  780.0 8.2 copy-start.22
  840.4 267.7 %copy-start.28 = (f32[2048]{0:T(1024)S(1)}, f32[2048]{0:T(1024)}, u32[]{:S(2)}) copy-start(f32[2048]{0:T(1024)} %param.19) | copy-start | bytes 24580
  878.2 278.8 %copy-start.1 = (bf16[256,2048]{1,0:T(8,128)(2,1)S(1)}, bf16[256,2048]{1,0:T(8,128)(2,1)}, u32[]{:S(2)}) copy-start(bf16[256,2048]{1,0:T(8,128)(2,1)} %param.23) | copy-start | bytes 3145732
  (35 other events, 162.1 us)
Sparse Core Ops, SparseCore 0:
  203.4 133.1 all-reduce.5
  338.6 54.5 all-gather.1
  441.1 126.5 all-reduce.7
  607.9 27.3 reduce-scatter.18
  715.7 27.3 reduce-scatter.12
  745.8 25.7 reduce-scatter.14
  774.6 25.7 reduce-scatter.16
  802.7 75.4 reduce-scatter.20
  880.6 77.2 reduce-scatter.22
  961.2 71.7 reduce-scatter.8
  1036.9 71.2 reduce-scatter.10
